TPU v7x, 32 devices: a whole 2x2x4 slice. The times are simulated.
32 devices in a mesh: grp: 4 (over x, core), seq: 8 (over z, y).
Axes of the slice: x: 2, y: 2, z: 4, core: 2. Of those that a mesh axis runs over, the one named last changes fastest.
Arguments:
- tokens: bfloat16 [32, 64, 128, 512], P(None, 'grp', 'seq'), may hold values from -6 to 6
- cotangent: bfloat16 [32, 64, 128, 512], P(None, 'grp', 'seq'), may hold values from -6 to 6
- gate_weight: bfloat16 [512, 512], replicated, may hold values from -0.25 to 0.25
- first_factor: bfloat16 [4, 32, 32], replicated, may hold values from -1 to 1
- middle_factor: bfloat16 [4, 64, 64], replicated, may hold values from -0.75 to 0.75
- last_factor: bfloat16 [4, 128, 128], replicated, may hold values from -0.5 to 0.5
Outputs:
- d_tokens: bfloat16 [32, 64, 128, 512], P(None, 'grp', 'seq')
- grad_gate: float32 [512, 512], P('seq')
- grad_first: float32 [4, 32, 32], replicated
- grad_middle: float32 [4, 64, 64], P(None, 'grp')
- grad_last: float32 [4, 128, 128], P(None, 'seq')
All inputs are finite; a program needn't handle non-finite values.
Results may differ from a plain program's by a relative error of at most 0.0065.
Values may be sent and summed in bfloat16 or wider, within the bound.
No kernel may reach another device: no remote copies, remote signals or barrier semaphores. Data moves between devices by JAX's collectives and lax.ppermute only.
A program may use at most 192 MiB of HBM per device.

v0:
```python
import math
import jax
import jax.numpy as jnp
from jax import lax
from jax.sharding import PartitionSpec as P

HEADS = 4


def headed(values):
    return values.reshape(values.shape[:-1] + (HEADS, values.shape[-1] // HEADS))


def mixing(weights, values, form):
    result = jnp.einsum(form, weights, headed(values), preferred_element_type=jnp.float32)
    return result.reshape(values.shape)


def contract(left, right, form):
    return jnp.einsum(form, headed(left), headed(right), preferred_element_type=jnp.float32)


def send_last(values):
    return lax.all_to_all(values, "seq", split_axis=0, concat_axis=2, tiled=True)


def send_middle(values):
    return lax.all_to_all(values, "grp", split_axis=2, concat_axis=1, tiled=True)


def return_middle(values):
    return lax.all_to_all(values, "grp", split_axis=1, concat_axis=2, tiled=True)


def return_last(values):
    return lax.all_to_all(values, "seq", split_axis=2, concat_axis=0, tiled=True)


def shards(tokens, cotangent, gate_weight, first_factor, middle_factor, last_factor):
    width = tokens.shape[-1]
    rows = tokens.reshape(-1, width)
    gate = jax.nn.sigmoid(jnp.dot(rows, gate_weight, preferred_element_type=jnp.float32)).reshape(
        tokens.shape
    )
    first_out = mixing(first_factor, tokens, "hab,bjkhe->ajkhe").astype(jnp.bfloat16)
    last_in = send_last(first_out)
    last_out = mixing(last_factor, last_in, "hab,ijbhe->ijahe").astype(jnp.bfloat16)
    middle_in = send_middle(last_out)
    middle_out = mixing(middle_factor, middle_in, "hab,ibkhe->iakhe").astype(jnp.bfloat16)
    mixer = return_last(return_middle(middle_out))
    upstream = cotangent.astype(jnp.float32)
    d_mix = (upstream * gate).astype(jnp.bfloat16)
    d_pre = (upstream * mixer.astype(jnp.float32) * gate * (1.0 - gate)).astype(jnp.bfloat16)
    pre_rows = d_pre.reshape(-1, width)
    gate_part = jnp.einsum("tc,td->cd", rows, pre_rows, preferred_element_type=jnp.float32)
    gate_term = jnp.einsum("td,cd->tc", pre_rows, gate_weight, preferred_element_type=jnp.float32)
    middle_grad_in = send_middle(send_last(d_mix))
    middle_back = mixing(middle_factor, middle_grad_in, "hba,ibkhe->iakhe").astype(jnp.bfloat16)
    middle_part = contract(middle_grad_in, middle_in, "iakhe,ibkhe->hab")
    last_back_in = return_middle(middle_back)
    last_back = mixing(last_factor, last_back_in, "hba,ijbhe->ijahe").astype(jnp.bfloat16)
    last_part = contract(last_back_in, last_in, "ijahe,ijbhe->hab")
    first_back_in = return_last(last_back)
    first_back = mixing(first_factor, first_back_in, "hba,bjkhe->ajkhe")
    first_part = contract(first_back_in, tokens, "ajkhe,bjkhe->hab")
    d_tokens = (
        (first_back.reshape(-1, width) + gate_term).astype(jnp.bfloat16).reshape(tokens.shape)
    )
    total = (
        tokens.shape[0]
        * tokens.shape[1]
        * tokens.shape[2]
        * lax.axis_size("grp")
        * lax.axis_size("seq")
    )
    factor = 1.0 / math.sqrt(total)
    gate_share, last_share = (
        lax.psum_scatter(gate_part, "seq", scatter_dimension=0, tiled=True),
        lax.psum_scatter(last_part, "seq", scatter_dimension=1, tiled=True),
    )
    middle_share = lax.psum_scatter(middle_part, "grp", scatter_dimension=1, tiled=True)
    gate_sum, last_sum, first_half = lax.psum((gate_share, last_share, first_part), "grp")
    middle_sum, first_sum = lax.psum((middle_share, first_half), "seq")
    return (d_tokens, gate_sum * factor, first_sum * factor, middle_sum * factor, last_sum * factor)


def solution(mesh):
    in_specs = (P(None, "grp", "seq", None), P(None, "grp", "seq", None), P(), P(), P(), P())
    out_specs = (
        P(None, "grp", "seq", None),
        P("seq", None),
        P(),
        P(None, "grp", None),
        P(None, "seq", None),
    )
    return jax.shard_map(shards, mesh=mesh, in_specs=in_specs, out_specs=out_specs, check_vma=False)
```

profile of v0, /device:TPU:0, one launch (start us, length us, event | category | flops | bytes accessed | tf_op | source)
XLA Modules:
  0.0 1805.6 jit_solution(3141081176804208275)
XLA Ops:
  7.2 12.5 reshape.70
  19.7 15.6 convert_bitcast_fusion.3
  35.4 28.2 %copy.134 = bf16[32,16,16,4,128]{4,3,2,1,0:T(4,128)(2,1)} copy(bf16[32,16,16,4,128]{4,0,2,1,3:T(8,128)(2,1)S(1)} %convert_bitcast_fusion.3) | data formatting | bytes 16777216 | tf_op jit(solution)/shard_map/convert_element_type | solution.py:45
  63.6 13.1 convert_element_type.79
  76.7 190.4 %all_to_all.120 = bf16[32,16,16,512]{3,2,1,0:T(8,128)(2,1)} all-to-all(bf16[32,16,16,512]{3,2,1,0:T(8,128)(2,1)} %convert_element_type.79), channel_id=1, replica_groups=mesh['grp'=4,'seq'=8] {'seq'}, dimensions={0} | all-to-all | bytes 16777216 | tf_op jit(solution)/shard_map/all_to_all | solution.py:24
  267.1 8.1 copy.229
  275.2 12.6 reshape.71
  287.8 9.5 convert_bitcast_fusion.2
  297.3 10.4 copy.137
  307.7 14.6 copy.138
  322.3 100.5 %all_to_all.121 = bf16[4,16,128,512]{3,1,0,2:T(8,128)(2,1)} all-to-all(bf16[4,16,128,512]{3,1,0,2:T(8,128)(2,1)} %copy.138), channel_id=1, replica_groups=mesh['grp'=4,'seq'=8] {'grp'}, dimensions={2} | all-to-all | bytes 16777216 | tf_op jit(solution)/shard_map/all_to_all | solution.py:28
  422.8 12.3 copy.140
  435.1 12.7 reshape.72
  447.9 14.9 convert_bitcast_fusion.1
  462.8 18.8 %copy.172 = bf16[4,64,32,4,128]{4,3,2,0,1:T(4,128)(2,1)} copy(bf16[4,64,32,4,128]{4,1,2,0,3:T(8,128)(2,1)S(1)} %convert_bitcast_fusion.1) | data formatting | bytes 16777216 | tf_op jit(solution)/shard_map/convert_element_type | solution.py:49
  481.6 13.1 reshape.87
  494.8 100.6 %all_to_all.122 = bf16[4,64,32,512]{3,2,0,1:T(8,128)(2,1)} all-to-all(bf16[4,64,32,512]{3,2,0,1:T(8,128)(2,1)} %reshape.87), channel_id=1, replica_groups=mesh['grp'=4,'seq'=8] {'grp'}, dimensions={1} | all-to-all | bytes 16777216 | tf_op jit(solution)/shard_map/all_to_all | solution.py:32
  595.3 8.3 copy.145
  603.6 11.3 copy.146
  614.9 5.1 all-to-all-start.7
  620.1 11.7 add_divide_fusion
  631.7 171.3 %all-to-all-done.7 = bf16[4,16,128,512]{3,1,0,2:T(8,128)(2,1)} async-done(((bf16[4,16,128,512]{3,1,0,2:T(8,128)(2,1)}), bf16[4,16,128,512]{3,1,0,2:T(8,128)(2,1)}, u32[]{:S(2)}, u32[]{:S(2)}) %all-to-all-start.7) | async-done | bytes 8388640 | tf_op jit(solution)/shard_map/all_to_all | solution.py:36
  803.0 11.4 copy.147
  814.4 11.4 convert_bitcast_fusion
  825.9 7.0 copy.148
  832.9 15.4 fusion.3
  848.3 188.7 %all_to_all.123 = bf16[32,16,16,512]{3,2,1,0:T(8,128)(2,1)} all-to-all(bf16[32,16,16,512]{3,2,1,0:T(8,128)(2,1)} %get-tuple-element.35), channel_id=1, replica_groups=mesh['grp'=4,'seq'=8] {'seq'}, dimensions={0} | all-to-all | bytes 16777216 | tf_op jit(solution)/shard_map/all_to_all | solution.py:24
  1037.0 8.1 copy.117
  1045.1 11.3 copy.118
  1056.5 100.5 %all_to_all.124 = bf16[4,16,128,512]{3,1,0,2:T(8,128)(2,1)} all-to-all(bf16[4,16,128,512]{3,1,0,2:T(8,128)(2,1)} %copy.118), channel_id=1, replica_groups=mesh['grp'=4,'seq'=8] {'grp'}, dimensions={2} | all-to-all | bytes 16777216 | tf_op jit(solution)/shard_map/all_to_all | solution.py:28
  1157.0 12.3 copy.231
  1169.3 12.7 reshape.67
  1182.0 17.9 convert_bitcast_fusion.5
  1199.9 12.1 copy.167
  1212.0 13.1 reshape.86
  1225.1 100.8 %all_to_all.125 = bf16[4,64,32,512]{3,2,0,1:T(8,128)(2,1)} all-to-all(bf16[4,64,32,512]{3,2,0,1:T(8,128)(2,1)} %reshape.86), channel_id=1, replica_groups=mesh['grp'=4,'seq'=8] {'grp'}, dimensions={1} | all-to-all | bytes 16777216 | tf_op jit(solution)/shard_map/all_to_all | solution.py:32
  1325.9 8.3 copy.230
  1334.1 12.6 reshape.68
  1346.7 9.5 convert_bitcast_fusion.4
  1356.2 10.3 copy.126
  1366.6 14.7 copy.127
  1381.2 5.0 all-to-all-start.3
  1386.3 9.5 convolution_bitcast_fusion.1
  1395.8 1.3 copy.174
  1397.2 189.2 %reduce-scatter.10.cloned.1.call-done = f32[64,512]{1,0:T(8,128)} async-done(((f32[512,512]{1,0:T(8,128)}), f32[64,512]{1,0:T(8,128)}) %reduce-scatter.10.cloned.1.call-update) | async-done | bytes 131088
  1586.4 1.8 copy.175
  1588.2 0.0 reduce-scatter.8.cloned.1.call-start
  1588.2 31.5 %all-reduce.4.cloned.1.call-done = f32[64,512]{0,1:T(8,128)} async-done(((f32[64,512]{0,1:T(8,128)}), f32[64,512]{0,1:T(8,128)}) %all-reduce.4.cloned.1.call-update) | async-done | bytes 131088 | tf_op jit(solution)/shard_map/psum | solution.py:82
  1619.7 1.0 broadcast_multiply_fusion
  1620.7 0.8 copy.155
  1621.5 8.8 fusion.35
  1630.3 0.5 reduce-scatter.6.cloned.1.call-start
  1630.8 15.2 fusion.40
  1646.0 15.4 copy.129
  1661.4 12.6 reshape.69
  1674.0 20.3 %convolution_bitcast_fusion = f32[32,16,16,4,128]{4,0,2,1,3:T(8,128)} fusion(bf16[32,16,16,4,128]{4,3,2,1,0:T(4,128)(2,1)} %reshape.69, bf16[4,32,32]{2,1,0:T(8,128)(2,1)S(1)} %copy-done.5), kind=kOutput, calls=%fused_computation.10 | convolution fusion | flops 268435456 | bytes 25174016 | tf_op jit(solution)/shard_map/hba,bjkhe->ajkhe/dot_general | solution.py:15
  1694.3 14.7 fusion.45
  1709.0 11.6 all-reduce.1
  1720.7 38.9 %all-reduce = (f32[4,32,32]{2,1,0:T(8,128)S(1)}, f32[4,16,64]{2,1,0:T(8,128)S(1)}) all-reduce(f32[4,32,32]{2,1,0:T(8,128)S(1)} %get-tuple-element.32, f32[4,16,64]{2,1,0:T(8,128)} %reduce-scatter.6.cloned.1.call-done), channel_id=1, replica_groups=mesh['grp'=4,'seq'=8] {'seq'}, use_global_device_ids=true, to_apply=%region_3.0 | all-reduce | flops 8192 | bytes 65536 | tf_op jit(solution)/shard_map/psum | solution.py:83
  1759.6 0.6 broadcast_multiply_fusion.1
  1760.2 0.6 broadcast_multiply_fusion.3
  1760.8 0.6 broadcast_multiply_fusion.2
  1761.5 21.1 %copy.132 = f32[32,16,16,4,128]{4,3,2,1,0:T(4,128)} copy(f32[32,16,16,4,128]{4,0,2,1,3:T(8,128)} %convolution_bitcast_fusion) | data formatting | bytes 33554432 | tf_op jit(solution)/shard_map/hba,bjkhe->ajkhe/transpose | solution.py:15
  1782.5 16.1 fusion.4
  (21 shorter events, 0.2 us)
Async XLA Ops:
  7.2 612.9 %copy-start = (bf16[512,512]{1,0:T(8,128)(2,1)S(1)}, bf16[512,512]{1,0:T(8,128)(2,1)}, u32[]{:S(2)}) copy-start(bf16[512,512]{1,0:T(8,128)(2,1)} %param.8) | copy-start | bytes 1572868
  7.2 12.6 copy-start.4
  275.2 12.6 copy-start.1
  435.1 12.7 copy-start.3
  614.9 188.1 %all-to-all-start.7 = ((bf16[4,16,128,512]{3,1,0,2:T(8,128)(2,1)}), bf16[4,16,128,512]{3,1,0,2:T(8,128)(2,1)}, u32[]{:S(2)}, u32[]{:S(2)}) async-start(bf16[4,16,128,512]{3,1,0,2:T(8,128)(2,1)} %copy.146), calls=%async_computation.7 | async-start | bytes 16777216 | tf_op jit(solution)/shard_map/all_to_all | solution.py:36
  1334.1 12.6 copy-start.2
  1381.2 264.8 %all-to-all-start.3 = ((bf16[4,16,128,512]{3,1,0,2:T(8,128)(2,1)}), bf16[4,16,128,512]{3,1,0,2:T(8,128)(2,1)}, u32[]{:S(2)}, u32[]{:S(2)}) async-start(bf16[4,16,128,512]{3,1,0,2:T(8,128)(2,1)} %copy.127), calls=%async_computation.3 | async-start | bytes 16777216 | tf_op jit(solution)/shard_map/all_to_all | solution.py:36
  1386.3 200.1 %reduce-scatter.10.cloned.1.call-start = ((), (), s32[]{:S(2)}) async-start(), calls=%async_computation.14 | async-start | bytes 1179648
  1397.2 222.6 %all-reduce.4.cloned.1.call-start = ((), (), s32[]{:S(2)}) async-start(), calls=%async_computation.11 | async-start | bytes 524288 | tf_op jit(solution)/shard_map/psum | solution.py:82
  1588.2 120.9 %reduce-scatter.8.cloned.1.call-start = ((), (), s32[]{:S(2)}) async-start(), calls=%async_computation.13 | async-start | bytes 294912 | tf_op jit(solution)/shard_map/reduce_scatter | solution.py:79
  1630.3 90.4 %reduce-scatter.6.cloned.1.call-start = ((), (), s32[]{:S(2)}) async-start(), calls=%async_computation.12 | async-start | bytes 163840 | tf_op jit(solution)/shard_map/reduce_scatter | solution.py:81
  1661.4 12.6 copy-start.5
Sparse Core Ops, SparseCore 0:
  1397.3 189.0 reduce-scatter.9
  1588.7 30.9 all-reduce.3
  1630.4 62.5 reduce-scatter.7
  1695.2 18.7 reduce-scatter.5
where the time goes:
time: 1820 us; the launch traced here: 1810 us
  blocking collectives  832 us (46%)
  waiting for transfers between devices  392 us (22%)
  local copies, waits for them, and re-layouts  363 us (20%)
  matrix products  164 us (9%)
  other arithmetic  29.7 us (2%)
    all_to_all x2, blocking collectives, send_last(): lax.all_to_all(values, 'seq', split_axis=0, concat_axis=2, tiled=True)  379 us
    all_to_all x2, blocking collectives, return_middle(): lax.all_to_all(values, 'grp', split_axis=1, concat_axis=2, tiled=True)  201 us
    all_to_all x2, blocking collectives, send_middle(): lax.all_to_all(values, 'grp', split_axis=2, concat_axis=1, tiled=True)  201 us
    unnamed x5, waiting for transfers between devices  189 us
    all_to_all x2, waiting for transfers between devices, return_last(): lax.all_to_all(values, 'seq', split_axis=2, concat_axis=0, tiled=True)  171 us
    dot_general x6, matrix products, mixing(): jnp.einsum(form, weights, headed(values), preferred_element_type=jnp.floa...  87.8 us
    reshape x6, local copies, waits for them, and re-layouts, headed(): values.reshape(values.shape[:-1] + (HEADS, values.shape[-1] // HEADS))  75.7 us
    convert_element_type x2, local copies, waits for them, and re-layouts, shards(): mixing(first_factor, tokens, 'hab,bjkhe->ajkhe').astype(jnp.bfloat16)  41.3 us
  transfers between devices with their start and end apart: 6, of which 3 were waited for; matrix products, arithmetic and copies ran while one was open for 6% of the time, Pallas kernels for 0%

commit v1 on v0

--- a/solution.py
+++ b/solution.py
@@ -33,7 +33,10 @@
 
 
 def return_last(values):
-    return lax.all_to_all(values, "seq", split_axis=2, concat_axis=0, tiled=True)
+    return jnp.concatenate(
+        lax.all_to_all(jnp.stack(jnp.split(values, lax.axis_size("seq"), axis=2)), "seq", 0, 0),
+        axis=0,
+    )
 
 
 def shards(tokens, cotangent, gate_weight, first_factor, middle_factor, last_factor):

time: 1820 us -> 1880 us (1.033)
  local copies, waits for them, and re-layouts: 363 us -> 429 us
    another operation x0 -> x12, local copies, waits for them, and re-layouts: none -> 124 us  [the longest x11 111 us: return_last(): jnp.stack(jnp.split(values, lax.axis_size('seq'), axis=2))]
    all_to_all x2 -> x0, local copies, waits for them, and re-layouts: 26.8 us -> none  [return_last(): lax.all_to_all(values, 'seq', split_axis=2, concat_axis=0, tiled=True)]
    unnamed x15 -> x35, local copies, waits for them, and re-layouts: 3.86 us -> 29.6 us
    reshape x6 -> x5, local copies, waits for them, and re-layouts: 75.7 us -> 63.2 us  [headed(): values.reshape(values.shape[:-1] + (HEADS, values.shape[-1] // HEADS))]
  transfers between devices with their start and end apart: 6 -> 6, of which waited for: 3 -> 4; matrix products, arithmetic and copies ran while one was open for 6% -> 5% of each run, Pallas kernels for 0% -> 0%
where the time goes in v1:
time: 1880 us; the launch traced here: 1870 us
  blocking collectives  831 us (44%)
  local copies, waits for them, and re-layouts  429 us (23%)
  waiting for transfers between devices  400 us (21%)
  matrix products  164 us (9%)
    all_to_all x2, blocking collectives, send_last(): lax.all_to_all(values, 'seq', split_axis=0, concat_axis=2, tiled=True)  378 us
    all_to_all x2, blocking collectives, return_middle(): lax.all_to_all(values, 'grp', split_axis=1, concat_axis=2, tiled=True)  201 us
    all_to_all x2, blocking collectives, send_middle(): lax.all_to_all(values, 'grp', split_axis=2, concat_axis=1, tiled=True)  201 us
    unnamed x5, waiting for transfers between devices  189 us
    all_to_all x2, waiting for transfers between devices, return_last(): lax.all_to_all(jnp.stack(jnp.split(values, lax.axis_size('seq'), axis=2))...  171 us
    another operation x11, local copies, waits for them, and re-layouts, return_last(): jnp.stack(jnp.split(values, lax.axis_size('seq'), axis=2))  111 us
    dot_general x6, matrix products, mixing(): jnp.einsum(form, weights, headed(values), preferred_element_type=jnp.floa...  87.9 us
    reshape x5, local copies, waits for them, and re-layouts, headed(): values.reshape(values.shape[:-1] + (HEADS, values.shape[-1] // HEADS))  63.2 us
  transfers between devices with their start and end apart: 6, of which 4 were waited for; matrix products, arithmetic and copies ran while one was open for 5% of the time, Pallas kernels for 0%

profile of v1, /device:TPU:0, one launch (start us, length us, event | category | flops | bytes accessed | tf_op | source)
XLA Modules:
  0.0 1866.8 jit_solution(7707701483854337278)
XLA Ops:
  7.2 12.5 reshape.63
  19.7 15.6 convert_bitcast_fusion.2
  35.4 17.6 copy.99
  53.0 13.1 convert_element_type.73
  66.1 190.5 %all_to_all.106 = bf16[32,16,16,512]{3,2,1,0:T(8,128)(2,1)} all-to-all(bf16[32,16,16,512]{3,2,1,0:T(8,128)(2,1)} %convert_element_type.73), channel_id=1, replica_groups=mesh['grp'=4,'seq'=8] {'seq'}, dimensions={0} | all-to-all | bytes 16777216 | tf_op jit(solution)/shard_map/all_to_all | solution.py:24
  256.6 8.1 copy.190
  264.7 12.6 reshape.64
  277.3 9.5 convert_bitcast_fusion.1
  286.8 10.3 copy.102
  297.2 14.6 copy.103
  311.8 100.5 %all_to_all.107 = bf16[4,16,128,512]{3,1,0,2:T(8,128)(2,1)} all-to-all(bf16[4,16,128,512]{3,1,0,2:T(8,128)(2,1)} %copy.103), channel_id=1, replica_groups=mesh['grp'=4,'seq'=8] {'grp'}, dimensions={2} | all-to-all | bytes 16777216 | tf_op jit(solution)/shard_map/all_to_all | solution.py:28
  412.3 12.3 copy.105
  424.7 12.7 reshape.65
  437.4 14.9 convert_bitcast_fusion
  452.3 18.6 copy.133
  471.0 13.1 reshape.79
  484.1 100.5 %all_to_all.108 = bf16[4,64,32,512]{3,2,0,1:T(8,128)(2,1)} all-to-all(bf16[4,64,32,512]{3,2,0,1:T(8,128)(2,1)} %reshape.79), channel_id=1, replica_groups=mesh['grp'=4,'seq'=8] {'grp'}, dimensions={1} | all-to-all | bytes 16777216 | tf_op jit(solution)/shard_map/all_to_all | solution.py:32
  584.7 8.3 copy.110
  592.9 2.4 fusion.57
  595.4 3.0 fusion.56
  600.6 2.3 fusion.54
  607.2 4.9 all-to-all-start.7
  612.2 11.7 add_divide_fusion
  623.9 171.3 %all-to-all-done.7 = bf16[8,4,16,16,512]{4,3,2,1,0:T(8,128)(2,1)} async-done(((bf16[8,4,16,16,512]{4,3,2,1,0:T(8,128)(2,1)}), bf16[8,4,16,16,512]{4,3,2,1,0:T(8,128)(2,1)}, u32[]{:S(2)}, u32[]{:S(2)}) %all-to-all-start.7) | async-done | bytes 8388640 | tf_op jit(solution)/shard_map/all_to_all | solution.py:37
  795.2 15.0 fusion.3
  810.2 187.1 %all_to_all.109 = bf16[32,16,16,512]{3,2,1,0:T(8,128)(2,1)} all-to-all(bf16[32,16,16,512]{3,2,1,0:T(8,128)(2,1)S(1)} %get-tuple-element.30), channel_id=1, replica_groups=mesh['grp'=4,'seq'=8] {'seq'}, dimensions={0} | all-to-all | bytes 16777216 | tf_op jit(solution)/shard_map/all_to_all | solution.py:24
  997.3 8.1 copy.77
  1005.4 11.4 copy.78
  1016.7 100.5 %all_to_all.110 = bf16[4,16,128,512]{3,1,0,2:T(8,128)(2,1)} all-to-all(bf16[4,16,128,512]{3,1,0,2:T(8,128)(2,1)} %copy.78), channel_id=1, replica_groups=mesh['grp'=4,'seq'=8] {'grp'}, dimensions={2} | all-to-all | bytes 16777216 | tf_op jit(solution)/shard_map/all_to_all | solution.py:28
  1117.3 12.3 copy.192
  1129.6 12.7 reshape.61
  1142.3 17.9 convert_bitcast_fusion.4
  1160.2 12.1 copy.129
  1172.3 13.1 reshape.78
  1185.4 100.9 %all_to_all.111 = bf16[4,64,32,512]{3,2,0,1:T(8,128)(2,1)} all-to-all(bf16[4,64,32,512]{3,2,0,1:T(8,128)(2,1)} %reshape.78), channel_id=1, replica_groups=mesh['grp'=4,'seq'=8] {'grp'}, dimensions={1} | all-to-all | bytes 16777216 | tf_op jit(solution)/shard_map/all_to_all | solution.py:32
  1286.3 8.3 copy.191
  1294.6 12.5 reshape.62
  1307.1 9.5 convert_bitcast_fusion.3
  1316.6 10.3 copy.86
  1327.0 48.7 %slice_bitcast_fusion = (bf16[1,4,16,16,512]{3,4,2,1,0:T(8,128)(2,1)}, bf16[1,4,16,16,512]{3,4,2,1,0:T(8,128)(2,1)}, bf16[1,4,16,16,512]{3,4,2,1,0:T(8,128)(2,1)...) fusion(bf16[4,16,128,512]{2,3,1,0:T(8,128)(2,1)} %bitcast.166), kind=kLoop, calls=%fused_computation.10 | loop fusion | bytes 16777216 | tf_op jit(solution)/shard_map/stack | solution.py:37
  1375.7 6.7 copy.94
  1382.4 6.7 copy.93
  1389.1 7.8 copy.92
  1396.9 7.8 copy.91
  1404.7 7.8 copy.90
  1412.4 7.8 copy.89
  1420.3 7.8 copy.88
  1428.0 7.9 copy.87
  1436.0 2.4 constant_dynamic-update-slice_fusion.7
  1443.0 2.3 constant_dynamic-update-slice_fusion.4
  1449.5 4.9 all-to-all-start.3
  1454.5 9.5 convolution_bitcast_fusion.1
  1465.5 189.2 %reduce-scatter.10.cloned.1.call-done = f32[64,512]{1,0:T(8,128)} async-done(((f32[512,512]{1,0:T(8,128)}), f32[64,512]{1,0:T(8,128)}) %reduce-scatter.10.cloned.1.call-update) | async-done | bytes 131088
  1656.4 31.5 %all-reduce.4.cloned.1.call-done = f32[64,512]{0,1:T(8,128)} async-done(((f32[64,512]{0,1:T(8,128)}), f32[64,512]{0,1:T(8,128)}) %all-reduce.4.cloned.1.call-update) | async-done | bytes 131088 | tf_op jit(solution)/shard_map/psum | solution.py:85
  1689.7 8.8 fusion.35
  1698.6 15.2 fusion.40
  1713.8 12.8 reshape_reshape.7
  1726.6 20.4 %convolution_bitcast_fusion = f32[32,16,16,4,128]{4,0,2,1,3:T(8,128)} fusion(bf16[32,16,16,4,128]{4,3,2,1,0:T(4,128)(2,1)} %reshape_reshape.7, bf16[4,32,32]{2,1,0:T(8,128)(2,1)S(1)} %copy-done.8), kind=kOutput, calls=%fused_computation.9 | convolution fusion | flops 268435456 | bytes 25174016 | tf_op jit(solution)/shard_map/hba,bjkhe->ajkhe/dot_general | solution.py:15
  1747.0 14.9 fusion.45
  1762.0 12.1 all-reduce.1
  1774.1 8.2 reduce-scatter.6.cloned.1.call-done
  1782.2 38.8 %all-reduce = (f32[4,32,32]{2,1,0:T(8,128)S(1)}, f32[4,16,64]{2,1,0:T(8,128)S(1)}) all-reduce(f32[4,32,32]{2,1,0:T(8,128)S(1)} %get-tuple-element.27, f32[4,16,64]{2,1,0:T(8,128)} %reduce-scatter.6.cloned.1.call-done), channel_id=1, replica_groups=mesh['grp'=4,'seq'=8] {'seq'}, use_global_device_ids=true, to_apply=%region_3.0 | all-reduce | flops 8192 | bytes 65536 | tf_op jit(solution)/shard_map/psum | solution.py:86
  1822.9 21.1 %copy.97 = f32[32,16,16,4,128]{4,3,2,1,0:T(4,128)} copy(f32[32,16,16,4,128]{4,0,2,1,3:T(8,128)} %convolution_bitcast_fusion) | data formatting | bytes 33554432 | tf_op jit(solution)/shard_map/hba,bjkhe->ajkhe/transpose | solution.py:15
  1844.0 16.1 fusion.4
  (46 shorter events, 22.3 us)
Async XLA Ops:
  7.2 605.0 %copy-start = (bf16[512,512]{1,0:T(8,128)(2,1)S(1)}, bf16[512,512]{1,0:T(8,128)(2,1)}, u32[]{:S(2)}) copy-start(bf16[512,512]{1,0:T(8,128)(2,1)} %param.8) | copy-start | bytes 1572868
  7.2 12.6 copy-start.7
  264.7 12.6 copy-start.4
  424.7 12.7 copy-start.6
  592.9 10.0 copy-start.1
  607.2 187.9 %all-to-all-start.7 = ((bf16[8,4,16,16,512]{4,3,2,1,0:T(8,128)(2,1)}), bf16[8,4,16,16,512]{4,3,2,1,0:T(8,128)(2,1)}, u32[]{:S(2)}, u32[]{:S(2)}) async-start(bf16[8,4,16,16,512]{4,3,2,1,0:T(8,128)(2,1)} %fusion.50), calls=%async_computation.7 | async-start | bytes 16777216 | tf_op jit(solution)/shard_map/all_to_all | solution.py:37
  1294.6 12.5 copy-start.5
  1436.0 9.3 copy-start.3
  1436.0 10.4 copy-start.2
  1449.5 264.2 %all-to-all-start.3 = ((bf16[8,4,16,16,512]{4,3,2,1,0:T(8,128)(2,1)}), bf16[8,4,16,16,512]{4,3,2,1,0:T(8,128)(2,1)}, u32[]{:S(2)}, u32[]{:S(2)}) async-start(bf16[8,4,16,16,512]{4,3,2,1,0:T(8,128)(2,1)} %constant_dynamic-update-slice_fusion), calls=%async_computation.3 | async-start | bytes 16777216 | tf_op jit(solution)/shard_map/all_to_all | solution.py:37
  1454.5 200.1 %reduce-scatter.10.cloned.1.call-start = ((), (), s32[]{:S(2)}) async-start(), calls=%async_computation.14 | async-start | bytes 1179648
  1465.4 222.6 %all-reduce.4.cloned.1.call-start = ((), (), s32[]{:S(2)}) async-start(), calls=%async_computation.11 | async-start | bytes 524288 | tf_op jit(solution)/shard_map/psum | solution.py:85
  1656.4 105.6 %reduce-scatter.8.cloned.1.call-start = ((), (), s32[]{:S(2)}) async-start(), calls=%async_computation.13 | async-start | bytes 294912 | tf_op jit(solution)/shard_map/reduce_scatter | solution.py:82
  1698.5 83.7 %reduce-scatter.6.cloned.1.call-start = ((), (), s32[]{:S(2)}) async-start(), calls=%async_computation.12 | async-start | bytes 163840 | tf_op jit(solution)/shard_map/reduce_scatter | solution.py:84
  1713.8 12.8 copy-start.8
Sparse Core Ops, SparseCore 0:
  1465.5 189.0 reduce-scatter.9
  1656.9 30.9 all-reduce.3
  1698.7 62.5 reduce-scatter.7
  1763.5 18.6 reduce-scatter.5
